TPU v7x, 256 devices: a whole 4x4x8 slice. The times are simulated.
256 devices in a mesh: aa: 8 (over z), ba: 32 (over x, y, core).
Axes of the slice: x: 4, y: 4, z: 8, core: 2. Of those that a mesh axis runs over, the one named last changes fastest.
Arguments:
- deltas: bfloat16 [1048576, 128], P(('aa', 'ba')), may hold values from -6 to 6
- row_ids: int32 [1048576], P(('aa', 'ba')), may hold values from 0 to 4095, as said below
- sample_counts: int32 [1048576], P(('aa', 'ba')), may hold values from 1 to 8
- live: int32 [1048576], P(('aa', 'ba')), may hold values from 0 to 1, as said below
- table: float32 [1048576, 128], P(('aa', 'ba')), may hold values from -6 to 6
- accum: float32 [1048576, 128], P(('aa', 'ba')), may hold values from 0.01 to 1
Outputs:
- new_table: float32 [1048576, 128], P(('aa', 'ba'))
- new_accum: float32 [1048576, 128], P(('aa', 'ba'))
- fresh_rows: bfloat16 [1048576, 128], P(('aa', 'ba'))
Inputs may be any that keep to these rules, and one draw needn't show every extreme that they name: `row_ids`: A replica's 4096 slots are 256 blocks of 16; block j holds rows of owner j, given as offsets among its 4096 rows, pairwise distinct within the block. In each block of 16 slots the live ones come first; every replica has some block with all 16 slots live.
All inputs are finite; a program needn't handle non-finite values.
Results may differ from a plain program's by a relative error of at most 0.0012.
Values may be sent and summed in bfloat16 or wider, within the bound.
A program may use at most 64 MiB of HBM per device.

v0:
```python
import jax
import jax.numpy as jnp
from jax import lax
from jax.sharding import PartitionSpec as P

learn_rate = 0.1
epsilon = 1e-08


def split_up(shard, dim, length):
    before, after = (shard.shape[:dim], shard.shape[dim + 1 :])
    return jnp.moveaxis(shard.reshape(*before, length, -1, *after), dim, 0)


def in_order(tiles, dim):
    lengths = list(tiles.shape[1:])
    lengths[dim] *= tiles.shape[0]
    return jnp.moveaxis(tiles, 0, dim).reshape(lengths)


def joined_exchange(shard, axis, axes, splits, concats):
    sizes = [lax.axis_size(a) for a in axes]
    tiles = split_up(shard, splits[0], sizes[0])
    tiles = jnp.moveaxis(split_up(tiles, splits[1] + 1, sizes[1]), 0, 1)
    inside = tiles.shape[2:]
    tiles = tiles.reshape(-1, *inside)
    tiles = lax.all_to_all(tiles, axis, split_axis=0, concat_axis=0, tiled=True)
    tiles = in_order(tiles.reshape(*sizes, *inside), concats[0] + 1)
    return in_order(tiles, concats[1])


def on_device(deltas, row_ids, sample_counts, live, table, accum):
    n_first = lax.axis_size("aa")
    n_second = lax.axis_size("ba")
    width = deltas.shape[1]
    rows_owned = table.shape[0]
    slot_cap = deltas.shape[0] // (n_first * n_second)
    grid = (n_first, n_second, slot_cap)
    blocks = deltas.reshape(n_first, n_second, slot_cap, width)
    ids = row_ids.reshape(grid)
    payload = (blocks, ids, (sample_counts * live).reshape(grid))
    arrived = (
        joined_exchange(payload[0], ("aa", "ba"), ("aa", "ba"), (0, 1), (0, 1)),
        joined_exchange(payload[1], ("aa", "ba"), ("aa", "ba"), (0, 1), (0, 1)),
        joined_exchange(payload[2], ("aa", "ba"), ("aa", "ba"), (0, 1), (0, 1)),
    )
    got_rows, got_ids, got_weight = arrived
    local = got_ids.reshape(-1).astype(jnp.int32)
    weight = got_weight.reshape(-1).astype(jnp.float32)
    slot_rows = got_rows.reshape(-1, width)
    block_len = min(512, rows_owned)
    n_blocks = rows_owned // block_len
    table_blocks = table.reshape(n_blocks, block_len, width)
    accum_blocks = accum.reshape(n_blocks, block_len, width)
    offsets = jnp.arange(n_blocks, dtype=jnp.int32) * block_len
    within = jnp.arange(block_len, dtype=jnp.int32)
    contract = (((0,), (0,)), ((), ()))

    def owner_block(replies, inputs):
        start, table_part, accum_part = inputs
        matched = local[:, None] == (start + within)[None, :]
        weighted = jnp.where(matched, weight[:, None], 0.0)
        numer = lax.dot_general(
            weighted.astype(jnp.bfloat16), slot_rows, contract, preferred_element_type=jnp.float32
        )
        total = jnp.sum(weighted, axis=0)
        grad = numer / jnp.maximum(total, 1.0)[:, None]
        accum_next = accum_part + grad * grad
        table_next = table_part - learn_rate * grad / (jnp.sqrt(accum_next) + epsilon)
        upper = table_next.astype(jnp.bfloat16)
        lower = (table_next - upper.astype(jnp.float32)).astype(jnp.bfloat16)
        picker = matched.astype(jnp.bfloat16)
        picked = jnp.dot(picker, upper, preferred_element_type=jnp.float32) + jnp.dot(
            picker, lower, preferred_element_type=jnp.float32
        )
        return (replies + picked, (table_next, accum_next))

    start_replies = jnp.zeros((local.shape[0], width), jnp.float32)
    gathered, updated = lax.scan(owner_block, start_replies, (offsets, table_blocks, accum_blocks))
    new_table = updated[0].reshape(rows_owned, width)
    new_accum = updated[1].reshape(rows_owned, width)
    replies = gathered.astype(jnp.bfloat16).reshape(n_first, n_second, slot_cap, width)
    returned = joined_exchange(replies, ("aa", "ba"), ("aa", "ba"), (0, 1), (0, 1))
    return (new_table, new_accum, returned.reshape(-1, width))


def solution(mesh):
    placed = (
        P(("aa", "ba"), None),
        P(("aa", "ba")),
        P(("aa", "ba")),
        P(("aa", "ba")),
        P(("aa", "ba"), None),
        P(("aa", "ba"), None),
    )
    return jax.shard_map(
        on_device,
        mesh=mesh,
        in_specs=placed,
        out_specs=(P(("aa", "ba"), None), P(("aa", "ba"), None), P(("aa", "ba"), None)),
        check_vma=False,
    )
```

profile of v0, /device:TPU:1, one launch (start us, length us, event | category | flops | bytes accessed | tf_op | source)
XLA Modules:
  0.0 212.1 jit_solution(1016824634889490163)
XLA Ops:
  2.1 15.7 %all-to-all-start.1 = ((s32[256,1,1,16]{3,2,1,0:T(1,128)}), s32[256,1,1,16]{3,2,1,0:T(1,128)S(1)}, u32[]{:S(2)}, u32[]{:S(2)}) async-start(s32[256,1,1,16]{3,2,1,0:T(1,128)} %bitcast.6), calls=%async_computation.1 | async-start | bytes 262144 | tf_op jit(solution)/shard_map/all_to_all | solution.py:27
  18.6 12.1 %all-to-all-done.1 = s32[256,1,1,16]{3,2,1,0:T(1,128)S(1)} async-done(((s32[256,1,1,16]{3,2,1,0:T(1,128)}), s32[256,1,1,16]{3,2,1,0:T(1,128)S(1)}, u32[]{:S(2)}, u32[]{:S(2)}) %all-to-all-start.1) | async-done | bytes 16416 | tf_op jit(solution)/shard_map/all_to_all | solution.py:27
  30.7 18.3 %all_to_all.20 = s32[256,1,1,16]{3,2,1,0:T(1,128)S(1)} all-to-all(s32[256,1,1,16]{3,2,1,0:T(1,128)S(1)} %bitcast.77), channel_id=1, replica_groups=mesh['aa'=8,'ba'=32] {'aa','ba'}, dimensions={0} | all-to-all | bytes 32768 | tf_op jit(solution)/shard_map/all_to_all | solution.py:27
  49.0 5.5 %all-to-all-start.2 = ((bf16[256,1,1,16,128]{4,3,2,1,0:T(8,128)(2,1)}), bf16[256,1,1,16,128]{4,3,2,1,0:T(8,128)(2,1)S(1)}, u32[]{:S(2)}, u32[]{:S(2)}) async-start(bf16[256,1,1,16,128]{4,3,2,1,0:T(8,128)(2,1)} %bitcast.74), calls=%async_computation.2 | async-start | bytes 2097152 | tf_op jit(solution)/shard_map/all_to_all | solution.py:27
  55.6 29.6 %all-to-all-done.2 = bf16[256,1,1,16,128]{4,3,2,1,0:T(8,128)(2,1)S(1)} async-done(((bf16[256,1,1,16,128]{4,3,2,1,0:T(8,128)(2,1)}), bf16[256,1,1,16,128]{4,3,2,1,0:T(8,128)(2,1)S(1)}, u32[]{:S(2)}, u32[]{:S(2)}) %all-to-all-start.2) | async-done | bytes 1048608 | tf_op jit(solution)/shard_map/all_to_all | solution.py:27
  85.2 88.9 %while.16 = (s32[]{:T(128)}, f32[4096,128]{1,0:T(8,128)S(1)}, f32[8,512,128]{2,1,0:T(8,128)}, f32[8,512,128]{2,1,0:T(8,128)}, s32[8,32,1,16]{3,1,0,2:T(8,128)}, ...) while((s32[]{:T(128)}, f32[4096,128]{1,0:T(8,128)S(1)}, ...), condition=%wide.wide.region_2.3_spmd.clone, body=%wide.wide.region_0.2_spmd.clone.sunk | while | flops 1627652608 | bytes 11389091 | solution.py:79
  87.0 1.4 fusion.49
  88.4 4.3 %bitcast_dynamic-update-slice_fusion.4 = (f32[8,512,128]{2,1,0:T(8,128)}, f32[512,128]{1,0:T(8,128)S(1)}, f32[8,512,128]{2,1,0:T(8,128)}) fusion(f32[8,512,128]{2,1,0:T(8,128)} %get-tuple-element.284, s32[]{:T(128)S(6)} %copy.26, f32[8,512,128]{2,1,0:T(8,128)} %get-tuple-element.304, f32[8,512,128]{2,1,0:T(8,128)} %get-tuple-element.301, ...), kind=kOutput, calls=%fused_computation.21.clone.clone.1 | convolution fusion | flops 541523968 | bytes 2396164 | tf_op jit(solution)/shard_map/while/body/eval_jaxpr/dot_general | solution.py:63
  94.1 2.3 %fusion.51 = f32[4096,128]{1,0:T(8,128)S(1)} fusion(f32[4096,128]{1,0:T(8,128)S(1)} %fusion.50, s32[512]{0:T(512)S(1)} %iota_add_fusion.3, s32[4096]{0:T(1024)S(1)} %get-tuple-element.305, f32[4096,128]{1,0:T(8,128)S(1)} %get-tuple-element.283, pred[]{:T(512)S(6)} %compare.4, f32[512,128]{1,0:T(8,128)S(1)} %get-tuple-element.266), kind=kOutput, calls=%fused_computation.9.clone.clone.1 | convolution fusion | flops 540606464 | bytes 6572033 | tf_op jit(solution)/shard_map/while/body/eval_jaxpr/dot_general | solution.py:73
  98.1 1.4 fusion.49
  99.5 4.3 %bitcast_dynamic-update-slice_fusion.4 = (f32[8,512,128]{2,1,0:T(8,128)}, f32[512,128]{1,0:T(8,128)S(1)}, f32[8,512,128]{2,1,0:T(8,128)}) fusion(f32[8,512,128]{2,1,0:T(8,128)} %get-tuple-element.284, s32[]{:T(128)S(6)} %copy.26, f32[8,512,128]{2,1,0:T(8,128)} %get-tuple-element.304, f32[8,512,128]{2,1,0:T(8,128)} %get-tuple-element.301, ...), kind=kOutput, calls=%fused_computation.21.clone.clone.1 | convolution fusion | flops 541523968 | bytes 2396164 | tf_op jit(solution)/shard_map/while/body/eval_jaxpr/dot_general | solution.py:63
  105.2 2.3 %fusion.51 = f32[4096,128]{1,0:T(8,128)S(1)} fusion(f32[4096,128]{1,0:T(8,128)S(1)} %fusion.50, s32[512]{0:T(512)S(1)} %iota_add_fusion.3, s32[4096]{0:T(1024)S(1)} %get-tuple-element.305, f32[4096,128]{1,0:T(8,128)S(1)} %get-tuple-element.283, pred[]{:T(512)S(6)} %compare.4, f32[512,128]{1,0:T(8,128)S(1)} %get-tuple-element.266), kind=kOutput, calls=%fused_computation.9.clone.clone.1 | convolution fusion | flops 540606464 | bytes 6572033 | tf_op jit(solution)/shard_map/while/body/eval_jaxpr/dot_general | solution.py:73
  109.2 1.4 fusion.49
  110.6 4.3 %bitcast_dynamic-update-slice_fusion.4 = (f32[8,512,128]{2,1,0:T(8,128)}, f32[512,128]{1,0:T(8,128)S(1)}, f32[8,512,128]{2,1,0:T(8,128)}) fusion(f32[8,512,128]{2,1,0:T(8,128)} %get-tuple-element.284, s32[]{:T(128)S(6)} %copy.26, f32[8,512,128]{2,1,0:T(8,128)} %get-tuple-element.304, f32[8,512,128]{2,1,0:T(8,128)} %get-tuple-element.301, ...), kind=kOutput, calls=%fused_computation.21.clone.clone.1 | convolution fusion | flops 541523968 | bytes 2396164 | tf_op jit(solution)/shard_map/while/body/eval_jaxpr/dot_general | solution.py:63
  114.9 1.4 fusion.50
  116.3 2.3 %fusion.51 = f32[4096,128]{1,0:T(8,128)S(1)} fusion(f32[4096,128]{1,0:T(8,128)S(1)} %fusion.50, s32[512]{0:T(512)S(1)} %iota_add_fusion.3, s32[4096]{0:T(1024)S(1)} %get-tuple-element.305, f32[4096,128]{1,0:T(8,128)S(1)} %get-tuple-element.283, pred[]{:T(512)S(6)} %compare.4, f32[512,128]{1,0:T(8,128)S(1)} %get-tuple-element.266), kind=kOutput, calls=%fused_computation.9.clone.clone.1 | convolution fusion | flops 540606464 | bytes 6572033 | tf_op jit(solution)/shard_map/while/body/eval_jaxpr/dot_general | solution.py:73
  120.3 1.4 fusion.49
  121.8 4.3 %bitcast_dynamic-update-slice_fusion.4 = (f32[8,512,128]{2,1,0:T(8,128)}, f32[512,128]{1,0:T(8,128)S(1)}, f32[8,512,128]{2,1,0:T(8,128)}) fusion(f32[8,512,128]{2,1,0:T(8,128)} %get-tuple-element.284, s32[]{:T(128)S(6)} %copy.26, f32[8,512,128]{2,1,0:T(8,128)} %get-tuple-element.304, f32[8,512,128]{2,1,0:T(8,128)} %get-tuple-element.301, ...), kind=kOutput, calls=%fused_computation.21.clone.clone.1 | convolution fusion | flops 541523968 | bytes 2396164 | tf_op jit(solution)/shard_map/while/body/eval_jaxpr/dot_general | solution.py:63
  127.4 2.3 %fusion.51 = f32[4096,128]{1,0:T(8,128)S(1)} fusion(f32[4096,128]{1,0:T(8,128)S(1)} %fusion.50, s32[512]{0:T(512)S(1)} %iota_add_fusion.3, s32[4096]{0:T(1024)S(1)} %get-tuple-element.305, f32[4096,128]{1,0:T(8,128)S(1)} %get-tuple-element.283, pred[]{:T(512)S(6)} %compare.4, f32[512,128]{1,0:T(8,128)S(1)} %get-tuple-element.266), kind=kOutput, calls=%fused_computation.9.clone.clone.1 | convolution fusion | flops 540606464 | bytes 6572033 | tf_op jit(solution)/shard_map/while/body/eval_jaxpr/dot_general | solution.py:73
  131.4 1.4 fusion.49
  132.9 4.3 %bitcast_dynamic-update-slice_fusion.4 = (f32[8,512,128]{2,1,0:T(8,128)}, f32[512,128]{1,0:T(8,128)S(1)}, f32[8,512,128]{2,1,0:T(8,128)}) fusion(f32[8,512,128]{2,1,0:T(8,128)} %get-tuple-element.284, s32[]{:T(128)S(6)} %copy.26, f32[8,512,128]{2,1,0:T(8,128)} %get-tuple-element.304, f32[8,512,128]{2,1,0:T(8,128)} %get-tuple-element.301, ...), kind=kOutput, calls=%fused_computation.21.clone.clone.1 | convolution fusion | flops 541523968 | bytes 2396164 | tf_op jit(solution)/shard_map/while/body/eval_jaxpr/dot_general | solution.py:63
  138.5 2.3 %fusion.51 = f32[4096,128]{1,0:T(8,128)S(1)} fusion(f32[4096,128]{1,0:T(8,128)S(1)} %fusion.50, s32[512]{0:T(512)S(1)} %iota_add_fusion.3, s32[4096]{0:T(1024)S(1)} %get-tuple-element.305, f32[4096,128]{1,0:T(8,128)S(1)} %get-tuple-element.283, pred[]{:T(512)S(6)} %compare.4, f32[512,128]{1,0:T(8,128)S(1)} %get-tuple-element.266), kind=kOutput, calls=%fused_computation.9.clone.clone.1 | convolution fusion | flops 540606464 | bytes 6572033 | tf_op jit(solution)/shard_map/while/body/eval_jaxpr/dot_general | solution.py:73
  142.6 1.4 fusion.49
  144.0 4.3 %bitcast_dynamic-update-slice_fusion.4 = (f32[8,512,128]{2,1,0:T(8,128)}, f32[512,128]{1,0:T(8,128)S(1)}, f32[8,512,128]{2,1,0:T(8,128)}) fusion(f32[8,512,128]{2,1,0:T(8,128)} %get-tuple-element.284, s32[]{:T(128)S(6)} %copy.26, f32[8,512,128]{2,1,0:T(8,128)} %get-tuple-element.304, f32[8,512,128]{2,1,0:T(8,128)} %get-tuple-element.301, ...), kind=kOutput, calls=%fused_computation.21.clone.clone.1 | convolution fusion | flops 541523968 | bytes 2396164 | tf_op jit(solution)/shard_map/while/body/eval_jaxpr/dot_general | solution.py:63
  149.6 2.3 %fusion.51 = f32[4096,128]{1,0:T(8,128)S(1)} fusion(f32[4096,128]{1,0:T(8,128)S(1)} %fusion.50, s32[512]{0:T(512)S(1)} %iota_add_fusion.3, s32[4096]{0:T(1024)S(1)} %get-tuple-element.305, f32[4096,128]{1,0:T(8,128)S(1)} %get-tuple-element.283, pred[]{:T(512)S(6)} %compare.4, f32[512,128]{1,0:T(8,128)S(1)} %get-tuple-element.266), kind=kOutput, calls=%fused_computation.9.clone.clone.1 | convolution fusion | flops 540606464 | bytes 6572033 | tf_op jit(solution)/shard_map/while/body/eval_jaxpr/dot_general | solution.py:73
  153.7 1.4 fusion.49
  155.1 4.3 %bitcast_dynamic-update-slice_fusion.4 = (f32[8,512,128]{2,1,0:T(8,128)}, f32[512,128]{1,0:T(8,128)S(1)}, f32[8,512,128]{2,1,0:T(8,128)}) fusion(f32[8,512,128]{2,1,0:T(8,128)} %get-tuple-element.284, s32[]{:T(128)S(6)} %copy.26, f32[8,512,128]{2,1,0:T(8,128)} %get-tuple-element.304, f32[8,512,128]{2,1,0:T(8,128)} %get-tuple-element.301, ...), kind=kOutput, calls=%fused_computation.21.clone.clone.1 | convolution fusion | flops 541523968 | bytes 2396164 | tf_op jit(solution)/shard_map/while/body/eval_jaxpr/dot_general | solution.py:63
  160.7 2.3 %fusion.51 = f32[4096,128]{1,0:T(8,128)S(1)} fusion(f32[4096,128]{1,0:T(8,128)S(1)} %fusion.50, s32[512]{0:T(512)S(1)} %iota_add_fusion.3, s32[4096]{0:T(1024)S(1)} %get-tuple-element.305, f32[4096,128]{1,0:T(8,128)S(1)} %get-tuple-element.283, pred[]{:T(512)S(6)} %compare.4, f32[512,128]{1,0:T(8,128)S(1)} %get-tuple-element.266), kind=kOutput, calls=%fused_computation.9.clone.clone.1 | convolution fusion | flops 540606464 | bytes 6572033 | tf_op jit(solution)/shard_map/while/body/eval_jaxpr/dot_general | solution.py:73
  164.8 1.4 fusion.49
  166.2 4.3 %bitcast_dynamic-update-slice_fusion.4 = (f32[8,512,128]{2,1,0:T(8,128)}, f32[512,128]{1,0:T(8,128)S(1)}, f32[8,512,128]{2,1,0:T(8,128)}) fusion(f32[8,512,128]{2,1,0:T(8,128)} %get-tuple-element.284, s32[]{:T(128)S(6)} %copy.26, f32[8,512,128]{2,1,0:T(8,128)} %get-tuple-element.304, f32[8,512,128]{2,1,0:T(8,128)} %get-tuple-element.301, ...), kind=kOutput, calls=%fused_computation.21.clone.clone.1 | convolution fusion | flops 541523968 | bytes 2396164 | tf_op jit(solution)/shard_map/while/body/eval_jaxpr/dot_general | solution.py:63
  171.8 2.3 %fusion.51 = f32[4096,128]{1,0:T(8,128)S(1)} fusion(f32[4096,128]{1,0:T(8,128)S(1)} %fusion.50, s32[512]{0:T(512)S(1)} %iota_add_fusion.3, s32[4096]{0:T(1024)S(1)} %get-tuple-element.305, f32[4096,128]{1,0:T(8,128)S(1)} %get-tuple-element.283, pred[]{:T(512)S(6)} %compare.4, f32[512,128]{1,0:T(8,128)S(1)} %get-tuple-element.266), kind=kOutput, calls=%fused_computation.9.clone.clone.1 | convolution fusion | flops 540606464 | bytes 6572033 | tf_op jit(solution)/shard_map/while/body/eval_jaxpr/dot_general | solution.py:73
  174.2 36.9 %all_to_all.21 = bf16[256,1,1,16,128]{4,3,2,1,0:T(8,128)(2,1)S(1)} all-to-all(bf16[256,1,1,16,128]{4,3,2,1,0:T(8,128)(2,1)S(1)} %bitcast.72), channel_id=1, replica_groups=mesh['aa'=8,'ba'=32] {'aa','ba'}, dimensions={0} | all-to-all | bytes 2097152 | tf_op jit(solution)/shard_map/all_to_all | solution.py:27
  (47 shorter events, 27.9 us)
Async XLA Ops:
  2.1 28.6 %all-to-all-start.1 = ((s32[256,1,1,16]{3,2,1,0:T(1,128)}), s32[256,1,1,16]{3,2,1,0:T(1,128)S(1)}, u32[]{:S(2)}, u32[]{:S(2)}) async-start(s32[256,1,1,16]{3,2,1,0:T(1,128)} %bitcast.6), calls=%async_computation.1 | async-start | bytes 262144 | tf_op jit(solution)/shard_map/all_to_all | solution.py:27
  49.0 36.2 %all-to-all-start.2 = ((bf16[256,1,1,16,128]{4,3,2,1,0:T(8,128)(2,1)}), bf16[256,1,1,16,128]{4,3,2,1,0:T(8,128)(2,1)S(1)}, u32[]{:S(2)}, u32[]{:S(2)}) async-start(bf16[256,1,1,16,128]{4,3,2,1,0:T(8,128)(2,1)} %bitcast.74), calls=%async_computation.2 | async-start | bytes 2097152 | tf_op jit(solution)/shard_map/all_to_all | solution.py:27
  55.5 29.8 %copy-start = (s32[8,32,1,16]{3,1,0,2:T(8,128)}, s32[8,32,1,16]{3,1,0,2:T(8,128)S(1)}, u32[]{:S(2)}) copy-start(s32[8,32,1,16]{3,1,0,2:T(8,128)S(1)} %copy.18) | copy-start | bytes 49156
where the time goes:
time: 213 us; the launch traced here: 212 us
  matrix products  63.2 us (30%)
  blocking collectives  55.2 us (26%)
  waiting for transfers between devices  41.7 us (20%)
  starting transfers between devices  21.2 us (10%)
  other arithmetic  17.2 us (8%)
  local copies, waits for them, and re-layouts  12.4 us (6%)
    all_to_all x2, blocking collectives, joined_exchange(): tiles = lax.all_to_all(tiles, axis, split_axis=0, concat_axis=0, tiled=True)  55.2 us
    all_to_all x2, waiting for transfers between devices, joined_exchange(): tiles = lax.all_to_all(tiles, axis, split_axis=0, concat_axis=0, tiled=True)  41.7 us
    dot_general x8, matrix products, owner_block(): lax.dot_general(weighted.astype(jnp.bfloat16), slot_rows, contract, prefe...  34.2 us
    all_to_all x2, starting transfers between devices, joined_exchange(): tiles = lax.all_to_all(tiles, axis, split_axis=0, concat_axis=0, tiled=True)  21.2 us
    dot_general x8, matrix products, owner_block(): jnp.dot(picker, upper, preferred_element_type=jnp.float32)  18.1 us
    reduce_sum x8, other arithmetic, owner_block(): total = jnp.sum(weighted, axis=0)  11.2 us
    dot_general x8, matrix products, owner_block(): jnp.dot(picker, lower, preferred_element_type=jnp.float32)  10.9 us
    dynamic_slice x8, local copies, waits for them, and re-layouts, on_device(): lax.scan(owner_block, start_replies, (offsets, table_blocks, accum_blocks))  9.5 us
  transfers between devices with their start and end apart: 2, of which 2 were waited for; matrix products, arithmetic and copies ran while one was open for 1% of the time, Pallas kernels for 0%

commit v1 on v0

v1 whole, which is shorter than its diff:
```python
import jax
import jax.numpy as jnp
from jax import lax
from jax.experimental import pallas as pl
from jax.experimental.pallas import tpu as pltpu
from jax.sharding import PartitionSpec as P

learn_rate = 0.1
epsilon = 1e-08
MESH = pl.DeviceIdType.MESH
DMA = pltpu.SemaphoreType.DMA


def offset(p):
    return (p + 1) // 2 * (2 * (p % 2) - 1)


def partner(b, k):
    core, y, x = b % 2, b // 2 % 4, b // 8
    return ((x + k // 8) % 4 * 4 + (y + k // 2 % 4) % 4) * 2 + (core + k % 2) % 2


def landed(ref, sem):
    pltpu.make_async_copy(ref, ref, sem).wait()


def send(src, dst, send_sem, recv_sem, a, b):
    pltpu.make_async_remote_copy(
        src, dst, send_sem, recv_sem, device_id=(a, b), device_id_type=MESH
    ).start()


def swap_blocks(m):
    row = lax.broadcasted_iota(jnp.int32, m.shape, 0)
    block = lax.broadcasted_iota(jnp.int32, m.shape, 1) // 16
    out = jnp.zeros_like(m)
    for d in range(8):
        t = m if d == 0 else pltpu.roll(pltpu.roll(m, 8 - d, 0), 16 * d, 1)
        out = jnp.where(block == (row + d) % 8, t, out)
    return out


def kernel(
    deltas, ids, counts, live, table, accum,
    new_table, new_accum, fresh,
    tab, acc, numer, upper, zbuf, got, rep, rbuf, id_src, id_mid, id_row, id_got, id_lane, id_col,
    tab_sem, acc_sem, tab_out, acc_out, own_sem, back_sem,
    id_zsend, id_zrecv, id_bsend, id_brecv,
    zsend, zrecv, bsend, brecv, rzsend, rzrecv, rbsend, rbrecv,
):
    a, b = lax.axis_index("aa"), lax.axis_index("ba")
    rows = tab.shape[0]
    load_tab = pltpu.make_async_copy(table, tab, tab_sem)
    load_acc = pltpu.make_async_copy(accum, acc, acc_sem)
    load_tab.start()
    load_acc.start()

    barrier = pltpu.get_barrier_semaphore()
    for d in range(1, 8):
        pl.semaphore_signal(barrier, inc=1, device_id=((a + d) % 8, b), device_id_type=MESH)

    def greet(k, _):
        pl.semaphore_signal(barrier, inc=1, device_id=(a, partner(b, k)), device_id_type=MESH)
        return 0

    lax.fori_loop(1, 32, greet, 0)
    packed = ids[...] + counts[...] * live[...] * 65536
    for i in range(8):
        id_src[i] = packed[4 * i : 4 * i + 4]
    pl.semaphore_wait(barrier, 38)

    def ids_along(p, _):
        pa = (a + offset(p) + 8) % 8
        send(id_src.at[pa], id_mid.at[p], id_zsend, id_zrecv, pa, b)
        return 0

    lax.fori_loop(1, 8, ids_along, 0)

    def deltas_along(p, _):
        pa = (a + offset(p) + 8) % 8
        send(deltas.at[pl.ds(32 * pa, 32)], zbuf.at[p - 1], zsend, zrecv.at[p], pa, b)
        return 0

    lax.fori_loop(1, 8, deltas_along, 0)
    id_mid[0] = id_src[a]

    def spread(src, p):
        pltpu.make_async_copy(src.at[b], got.at[32 * p + b], own_sem.at[p]).start()

        def one(k, _):
            pb = partner(b, k)
            send(src.at[pb], got.at[32 * p + b], bsend, brecv.at[p], a, pb)
            return 0

        lax.fori_loop(1, 32, one, 0)

    spread(deltas.at[pl.ds(32 * a, 32)], 0)
    landed(id_mid.at[pl.ds(1, 7)], id_zrecv)
    for r in range(4):
        id_row[8 * r : 8 * r + 8, 0, :] = swap_blocks(id_mid[:, r, :])

    def ids_across(k, _):
        pb = partner(b, k)
        send(id_row.at[pb], id_got.at[b], id_bsend, id_brecv, a, pb)
        return 0

    lax.fori_loop(1, 32, ids_across, 0)
    id_got[b] = id_row[b]
    numer[...] = jnp.zeros_like(numer)

    landed(zbuf.at[0], zrecv.at[1])
    spread(zbuf.at[0], 1)
    landed(id_got.at[pl.ds(0, 31)], id_brecv)
    for r in range(4):
        id_lane[:, 128 * r : 128 * r + 128] = swap_blocks(id_got[8 * r : 8 * r + 8, 0, :])

    def scatter(p):
        landed(got.at[pl.ds(0, 31)], brecv.at[p])
        landed(got.at[0], own_sem.at[p])
        both = id_lane[pl.ds(p, 1), :]
        row = both % 65536
        weight = (both // 65536).astype(jnp.float32)
        values = got[pl.ds(32 * p, 32)].reshape(512, 128)
        values = jnp.concatenate([values, jnp.ones_like(values)], axis=1)

        def block(i, _):
            base = pl.multiple_of(i * 256, 256)
            here = lax.broadcasted_iota(jnp.int32, (256, 512), 0) == row - base
            picks = jnp.where(here, weight, 0.0).astype(jnp.bfloat16)
            numer[pl.ds(base, 256), :] += jnp.dot(
                picks, values, preferred_element_type=jnp.float32
            )
            return 0

        lax.fori_loop(0, rows // 256, block, 0)

    def incoming(p, _):
        landed(zbuf.at[p - 1], zrecv.at[p])
        spread(zbuf.at[p - 1], p)
        scatter(p - 2)
        return 0

    lax.fori_loop(2, 8, incoming, 0)
    scatter(6)
    scatter(7)

    load_tab.wait()
    load_acc.wait()

    def update(i, _):
        at = pl.ds(pl.multiple_of(i * 256, 256), 256)
        grad = numer[at, 0:128] / jnp.maximum(numer[at, 128:256], 1.0)
        accum_next = acc[at, :] + grad * grad
        table_next = tab[at, :] - learn_rate * grad / (jnp.sqrt(accum_next) + epsilon)
        acc[at, :] = accum_next
        tab[at, :] = table_next
        upper[at, :] = table_next.astype(jnp.bfloat16)
        return 0

    lax.fori_loop(0, rows // 256, update, 0)
    store_tab = pltpu.make_async_copy(tab, new_table, tab_out)
    store_acc = pltpu.make_async_copy(acc, new_accum, acc_out)
    store_tab.start()
    store_acc.start()

    def gather(p):
        row = id_lane[pl.ds(p, 1), :] % 65536
        id_col[...] = jnp.broadcast_to(row, (128, 512)).T
        total = jnp.zeros((512, 128), jnp.float32)
        lane = lax.broadcasted_iota(jnp.int32, (512, 128), 1)
        column = id_col[...] - lane
        for k in range(rows // 256):
            picks = jnp.concatenate(
                [
                    jnp.where(column == 256 * k, 1.0, 0.0).astype(jnp.bfloat16),
                    jnp.where(column == 256 * k + 128, 1.0, 0.0).astype(jnp.bfloat16),
                ],
                axis=1,
            )
            total += jnp.dot(picks, upper[256 * k : 256 * k + 256, :], preferred_element_type=jnp.float32)
        rep[pl.ds(32 * p, 32)] = total.astype(jnp.bfloat16).reshape(32, 16, 128)

    def reply(p):
        gather(p)
        pa = (a - offset(p) + 8) % 8
        send(rep.at[pl.ds(32 * p, 32)], rbuf.at[p - 1], rzsend, rzrecv.at[p], pa, b)

    def deliver(src, p):
        owner = (a + offset(p) + 8) % 8
        pltpu.make_async_copy(src.at[b], fresh.at[32 * owner + b], back_sem).start()

        def one(k, _):
            pb = partner(b, k)
            send(src.at[pb], fresh.at[32 * owner + b], rbsend, rbrecv, a, pb)
            return 0

        lax.fori_loop(1, 32, one, 0)

    def first(i, _):
        reply(7 - i)
        return 0

    def later(i, _):
        reply(7 - i)
        p = 10 - i
        landed(rbuf.at[p - 1], rzrecv.at[p])
        deliver(rbuf.at[p - 1], p)
        return 0

    lax.fori_loop(0, 3, first, 0)
    lax.fori_loop(3, 7, later, 0)
    gather(0)
    deliver(rep.at[pl.ds(0, 32)], 0)

    def last(i, _):
        p = 3 - i
        landed(rbuf.at[p - 1], rzrecv.at[p])
        deliver(rbuf.at[p - 1], p)
        return 0

    lax.fori_loop(0, 3, last, 0)

    landed(id_src.at[pl.ds(0, 7)], id_zsend)
    landed(id_row.at[pl.ds(0, 31)], id_bsend)
    landed(zbuf, zsend)
    landed(rbuf, rzsend)
    landed(fresh.at[pl.ds(0, 8)], back_sem)
    for sem, ref in ((bsend, got), (rbsend, got), (rbrecv, fresh)):
        landed(ref.at[pl.ds(0, 248)], sem)
    store_tab.wait()
    store_acc.wait()


def on_device(deltas, row_ids, sample_counts, live, table, accum):
    rows, width = table.shape
    blocks = (256, 16, width)
    small = (32, 128)
    anywhere = pl.BlockSpec(memory_space=pl.ANY)
    vmem = pl.BlockSpec(memory_space=pltpu.VMEM)
    bf16, f32, i32 = jnp.bfloat16, jnp.float32, jnp.int32
    V = pltpu.VMEM
    new_table, new_accum, fresh = pl.pallas_call(
        kernel,
        name="exchange",
        out_shape=(
            jax.ShapeDtypeStruct((rows, width), f32),
            jax.ShapeDtypeStruct((rows, width), f32),
            jax.ShapeDtypeStruct(blocks, bf16),
        ),
        in_specs=[anywhere, vmem, vmem, vmem, anywhere, anywhere],
        out_specs=(anywhere, anywhere, anywhere),
        scratch_shapes=[
            V((rows, width), f32), V((rows, width), f32), V((rows, 2 * width), f32), V((rows, width), bf16),
            V((7, 32, 16, width), bf16), V(blocks, bf16), V(blocks, bf16), V((7, 32, 16, width), bf16),
            V((8, 4, 128), i32), V((8, 4, 128), i32), V((32, 1, 128), i32), V((32, 1, 128), i32),
            V((8, 512), i32), V((512, 128), i32),
            DMA, DMA, DMA, DMA, DMA((8,)), DMA,
            DMA, DMA, DMA, DMA,
            DMA, DMA((8,)), DMA, DMA((8,)), DMA, DMA((8,)), DMA, DMA,
        ],
        compiler_params=pltpu.CompilerParams(
            collective_id=1, has_side_effects=True, vmem_limit_bytes=48 << 20
        ),
    )(
        deltas.reshape(blocks), row_ids.reshape(small), sample_counts.reshape(small),
        live.reshape(small), table, accum,
    )
    return new_table, new_accum, fresh.reshape(-1, width)


def solution(mesh):
    rows, slots = P(("aa", "ba"), None), P(("aa", "ba"))
    return jax.shard_map(
        on_device,
        mesh=mesh,
        in_specs=(rows, slots, slots, slots, rows, rows),
        out_specs=(rows, rows, rows),
        check_vma=False,
    )
```

time: 213 us -> 105 us (0.49)
  Pallas kernels: 0 us -> 96.2 us
  matrix products: 63.2 us -> 0 us
  blocking collectives: 55.2 us -> 0 us
  waiting for transfers between devices: 41.7 us -> 0 us
  starting transfers between devices: 21.2 us -> 0 us
  other arithmetic: 17.2 us -> 0 us
  local copies, waits for them, and re-layouts: 12.4 us -> 8 us
    pallas_call x0 -> x1, Pallas kernels: none -> 96.2 us  [on_device(): pl.pallas_call(kernel, name='exchange', out_shape=(jax.ShapeDtypeStruct((...]
    dot_general x24 -> x0, matrix products: 63.2 us -> none  [the longest x8 34.2 us: owner_block(): lax.dot_general(weighted.astype(jnp.bfloat16), slot_rows, contract, prefe...]
    all_to_all x2 -> x0, blocking collectives: 55.2 us -> none  [joined_exchange(): tiles = lax.all_to_all(tiles, axis, split_axis=0, concat_axis=0, tiled=True)]
    all_to_all x2 -> x0, waiting for transfers between devices: 41.7 us -> none  [joined_exchange(): tiles = lax.all_to_all(tiles, axis, split_axis=0, concat_axis=0, tiled=True)]
    all_to_all x2 -> x0, starting transfers between devices: 21.2 us -> none  [joined_exchange(): tiles = lax.all_to_all(tiles, axis, split_axis=0, concat_axis=0, tiled=True)]
    reduce_sum x8 -> x0, other arithmetic: 11.2 us -> none  [owner_block(): total = jnp.sum(weighted, axis=0)]
    dynamic_slice x8 -> x0, local copies, waits for them, and re-layouts: 9.5 us -> none  [on_device(): lax.scan(owner_block, start_replies, (offsets, table_blocks, accum_blocks))]
    unnamed x4 -> x13, local copies, waits for them, and re-layouts: 1.08 us -> 8 us
  transfers between devices with their start and end apart: 2 -> 0, of which waited for: 2 -> 0; matrix products, arithmetic and copies ran while one was open for 1% -> 0% of each run, Pallas kernels for 0% -> 0%
where the time goes in v1:
time: 105 us
  Pallas kernels  96.2 us (92%)
  local copies, waits for them, and re-layouts  8 us (8%)
    pallas_call x1, Pallas kernels, on_device(): pl.pallas_call(kernel, name='exchange', out_shape=(jax.ShapeDtypeStruct((...  96.2 us
    unnamed x13, local copies, waits for them, and re-layouts  8 us

profile of v1, /device:TPU:1, one launch (start us, length us, event | category | flops | bytes accessed | tf_op | source)
XLA Modules:
  0.0 104.9 jit_solution(11863463371781180768)
XLA Ops:
  0.6 0.0 copy-start
  0.6 1.2 %copy-done = bf16[4096,128]{1,0:T(8,128)(2,1)S(1)} copy-done((bf16[4096,128]{1,0:T(8,128)(2,1)S(1)}, bf16[4096,128]{1,0:T(8,128)(2,1)}, u32[]{:S(2)}) %copy-start) | copy-done | bytes 1048600
  1.9 0.0 copy-start.1
  1.9 0.7 copy-done.1
  2.6 0.0 copy-start.2
  2.6 0.7 copy-done.2
  3.3 0.0 copy-start.3
  3.3 0.7 copy-done.3
  4.0 96.2 %exchange.1 = (f32[4096,128]{1,0:T(8,128)S(1)}, f32[4096,128]{1,0:T(8,128)}, bf16[256,16,128]{2,1,0:T(8,128)(2,1)S(1)}) custom-call(bf16[256,16,128]{2,1,0:T(8,128)(2,1)S(1)} %bitcast.5, s32[32,128]{1,0:T(8,128)S(1)} %bitcast.7, s32[32,128]{1,0:T(8,128)S(1)} %bitcast.8, s32[32,128]{1,0:T(8,128)S(1)} %bitcast.9, f32[4096,128]{1,0:T(8,128)} %table.1, ...), custom_call_target="tpu_custom_call" | custom-call | tf_op jit(solution)/shard_map/exchange/pallas_call | solution.py:242
  100.2 0.0 copy-start.4
  100.2 1.3 %copy.12 = f32[4096,128]{1,0:T(8,128)} copy(f32[4096,128]{1,0:T(8,128)S(1)} %get-tuple-element.12) | data formatting | bytes 4194304
  101.5 1.0 copy-done.4
  102.6 1.3 %copy.13 = f32[4096,128]{1,0:T(8,128)} copy(f32[4096,128]{1,0:T(8,128)S(1)} %copy-done.4) | data formatting | bytes 4194304
  103.9 1.0 copy.14
Async XLA Ops:
  0.6 1.2 %copy-start = (bf16[4096,128]{1,0:T(8,128)(2,1)S(1)}, bf16[4096,128]{1,0:T(8,128)(2,1)}, u32[]{:S(2)}) copy-start(bf16[4096,128]{1,0:T(8,128)(2,1)} %param.6) | copy-start | bytes 3145732
  1.9 0.7 copy-start.1
  2.6 0.7 copy-start.2
  3.3 0.7 copy-start.3
  100.2 2.3 %copy-start.4 = (f32[4096,128]{1,0:T(8,128)S(1)}, f32[4096,128]{1,0:T(8,128)}, u32[]{:S(2)}) copy-start(f32[4096,128]{1,0:T(8,128)} %get-tuple-element.13) | copy-start | bytes 6291460

commit v2 on v1

v2 whole, which is shorter than its diff:
```python
import jax
import jax.numpy as jnp
from jax import lax
from jax.experimental import pallas as pl
from jax.experimental.pallas import tpu as pltpu
from jax.sharding import PartitionSpec as P

learn_rate = 0.1
epsilon = 1e-08
MESH = pl.DeviceIdType.MESH
DMA = pltpu.SemaphoreType.DMA


def offset(p):
    return (p + 1) // 2 * (2 * (p % 2) - 1)


def partner(b, k):
    core, y, x = b % 2, b // 2 % 4, b // 8
    return ((x + k // 8) % 4 * 4 + (y + k // 2 % 4) % 4) * 2 + (core + k % 2) % 2


def partner_back(b, k):
    core, y, x = b % 2, b // 2 % 4, b // 8
    return ((x + 4 - k // 8) % 4 * 4 + (y + 4 - k // 2 % 4) % 4) * 2 + (core + k % 2) % 2


def landed(ref, sem):
    pltpu.make_async_copy(ref, ref, sem).wait()


def send(src, dst, send_sem, recv_sem, a, b):
    pltpu.make_async_remote_copy(
        src, dst, send_sem, recv_sem, device_id=(a, b), device_id_type=MESH
    ).start()


def swap_blocks(m):
    row = lax.broadcasted_iota(jnp.int32, m.shape, 0)
    block = lax.broadcasted_iota(jnp.int32, m.shape, 1) // 16
    out = jnp.zeros_like(m)
    for d in range(8):
        t = m if d == 0 else pltpu.roll(pltpu.roll(m, 8 - d, 0), 16 * d, 1)
        out = jnp.where(block == (row + d) % 8, t, out)
    return out


def kernel(
    deltas, ids, counts, live, table, accum,
    new_table, new_accum, fresh,
    src, tab, acc, numer, upper, got, rep, ints, id_src, id_mid, id_row, id_got, lows,
    in_sem, tab_sem, acc_sem, int_sem, tab_out, acc_out, own_sem, ready,
    id_zsend, id_zrecv, id_bsend, id_brecv, dsend, drecv, rsend, rrecv,
):
    a, b = lax.axis_index("aa"), lax.axis_index("ba")
    me = 32 * a + b
    rows = tab.shape[0]
    load_ints = [
        pltpu.make_async_copy(x, ints.at[i], int_sem.at[i]) for i, x in enumerate((ids, counts, live))
    ]
    load_src = pltpu.make_async_copy(deltas, src, in_sem)
    load_tab = pltpu.make_async_copy(table, tab, tab_sem)
    load_acc = pltpu.make_async_copy(accum, acc, acc_sem)
    for copy in (*load_ints, load_src, load_tab, load_acc):
        copy.start()

    barrier = pltpu.get_barrier_semaphore()
    for d in range(1, 8):
        pl.semaphore_signal(barrier, inc=1, device_id=((a + d) % 8, b), device_id_type=MESH)

    def greet(k, _):
        pl.semaphore_signal(barrier, inc=1, device_id=(a, partner(b, k)), device_id_type=MESH)
        return 0

    lax.fori_loop(1, 32, greet, 0)
    for copy in load_ints:
        copy.wait()
    packed = ints[0] + ints[1] * ints[2] * 65536
    for i in range(8):
        id_src[i] = packed[4 * i : 4 * i + 4]
    load_src.wait()
    pl.semaphore_wait(barrier, 38)
    for d in range(1, 8):
        pl.semaphore_signal(ready, inc=1, device_id=((a + d) % 8, b), device_id_type=MESH)

    def ids_along(p, _):
        pa = (a + offset(p) + 8) % 8
        send(id_src.at[pa], id_mid.at[p], id_zsend, id_zrecv, pa, b)
        return 0

    lax.fori_loop(1, 8, ids_along, 0)
    id_mid[0] = id_src[a]

    def deltas_to(k, p):
        pa, pb = (a + offset(p) + 8) % 8, partner(b, k)
        send(src.at[32 * pa + pb], got.at[8 * k + p], dsend, drecv.at[k // 4], pa, pb)

    def plane_near(p, _):
        deltas_to(0, p)
        return 0

    own = pltpu.make_async_copy(src.at[me], got.at[0], own_sem)
    own.start()
    lax.fori_loop(1, 8, plane_near, 0)
    pl.semaphore_wait(ready, 7)

    def plane(k, _):
        for p in (1, 2, 3, 4, 5, 6, 7, 0):
            deltas_to(k, p)
        return 0

    lax.fori_loop(1, 4, plane, 0)
    landed(id_mid.at[pl.ds(1, 7)], id_zrecv)
    for r in range(4):
        id_row[8 * r : 8 * r + 8, 0, :] = swap_blocks(id_mid[:, r, :])

    def ids_across(k, _):
        pb = partner(b, k)
        send(id_row.at[pb], id_got.at[k], id_bsend, id_brecv, a, pb)
        return 0

    lax.fori_loop(1, 32, ids_across, 0)
    id_got[0] = id_row[b]
    lax.fori_loop(4, 32, plane, 0)
    numer[...] = jnp.zeros_like(numer)
    landed(id_got.at[pl.ds(0, 31)], id_brecv)

    def scatter(g, count):
        landed(got.at[pl.ds(0, count)], drecv.at[g])
        lanes = [id_got[4 * g + i] for i in range(4)]
        both = jnp.concatenate(lanes, axis=1)
        row = both % 65536
        high = row // 256
        weight = (both // 65536).astype(jnp.float32)
        low = lax.broadcasted_iota(jnp.int32, (256, 512), 0) == row % 256
        lows[...] = jnp.where(low, 1.0, 0.0).astype(jnp.bfloat16)
        values = got[pl.ds(32 * g, 32)].reshape(512, 128)
        values = jnp.concatenate([values, jnp.ones_like(values)], axis=1)

        def block(i, _):
            base = pl.multiple_of(i * STEP, STEP)
            picks = []
            for j in range(STEP // 256):
                w = jnp.where(high == i * (STEP // 256) + j, weight, 0.0)
                w = jnp.broadcast_to(w, (16, 512)).astype(jnp.bfloat16)
                w = jnp.concatenate([w] * 16, axis=0)
                picks.append(lows[...] * w)
            numer[pl.ds(base, STEP), :] += jnp.dot(
                jnp.concatenate(picks, axis=0), values, preferred_element_type=jnp.float32
            )
            return 0

        lax.fori_loop(0, rows // STEP, block, 0)

    own.wait()
    scatter(0, 31)

    def incoming(g, _):
        scatter(g, 32)
        return 0

    lax.fori_loop(1, 8, incoming, 0)

    load_tab.wait()
    load_acc.wait()

    def update(i, _):
        at = pl.ds(pl.multiple_of(i * 256, 256), 256)
        grad = numer[at, 0:128] / jnp.maximum(numer[at, 128:256], 1.0)
        accum_next = acc[at, :] + grad * grad
        table_next = tab[at, :] - learn_rate * grad / (jnp.sqrt(accum_next) + epsilon)
        acc[at, :] = accum_next
        tab[at, :] = table_next
        upper[at, :] = table_next.astype(jnp.bfloat16)
        return 0

    lax.fori_loop(0, rows // 256, update, 0)
    store_tab = pltpu.make_async_copy(tab, new_table, tab_out)
    store_acc = pltpu.make_async_copy(acc, new_accum, acc_out)

    def gather(g):
        columns = [jnp.broadcast_to(id_got[4 * g + i] % 65536, (128, 128)).T for i in range(4)]
        row = jnp.concatenate(columns, axis=0)
        high = (row // 256).astype(jnp.float32).astype(jnp.bfloat16)
        lane = lax.broadcasted_iota(jnp.int32, (512, 128), 1)
        row = row % 256
        near = jnp.where(row == lane, 1.0, 0.0).astype(jnp.bfloat16)
        far = jnp.where(row == lane + 128, 1.0, 0.0).astype(jnp.bfloat16)
        low = jnp.concatenate([near, far], axis=1)
        high = jnp.concatenate([high, high], axis=1)
        zero = jnp.zeros_like(low)
        picks = jnp.concatenate(
            [jnp.where(high == float(k), low, zero) for k in range(rows // 256)], axis=1
        )
        total = jnp.dot(picks, upper[...], preferred_element_type=jnp.float32)
        rep[pl.ds(32 * g, 32)] = total.astype(jnp.bfloat16).reshape(32, 16, 128)

    def reply(k, p):
        pa, pb = (a - offset(p) + 8) % 8, partner_back(b, k)
        send(rep.at[8 * k + p], fresh.at[me], rsend, rrecv, pa, pb)

    def replies(k, _):
        for p in (1, 2, 3, 4, 5, 6, 7, 0):
            reply(k, p)
        return 0

    gather(0)
    back = pltpu.make_async_copy(rep.at[0], fresh.at[me], own_sem)
    back.start()
    for p in range(1, 8):
        reply(0, p)
    lax.fori_loop(1, 4, replies, 0)
    store_tab.start()
    store_acc.start()

    def outgoing(g, _):
        gather(g)
        lax.fori_loop(4 * g, 4 * g + 4, replies, 0)
        return 0

    lax.fori_loop(1, 8, outgoing, 0)

    landed(id_src.at[pl.ds(0, 7)], id_zsend)
    landed(id_row.at[pl.ds(0, 31)], id_bsend)
    back.wait()
    landed(got.at[pl.ds(0, 255)], dsend)
    landed(rep.at[pl.ds(0, 255)], rsend)
    landed(fresh.at[pl.ds(0, 255)], rrecv)
    store_tab.wait()
    store_acc.wait()


STEP = 1024


def on_device(deltas, row_ids, sample_counts, live, table, accum):
    rows, width = table.shape
    blocks = (256, 16, width)
    small = (32, 128)
    anywhere = pl.BlockSpec(memory_space=pl.ANY)
    hbm = pl.BlockSpec(memory_space=pltpu.HBM)
    bf16, f32, i32 = jnp.bfloat16, jnp.float32, jnp.int32
    V = pltpu.VMEM
    new_table, new_accum, fresh = pl.pallas_call(
        kernel,
        name="exchange",
        out_shape=(
            jax.ShapeDtypeStruct((rows, width), f32),
            jax.ShapeDtypeStruct((rows, width), f32),
            jax.ShapeDtypeStruct(blocks, bf16),
        ),
        in_specs=[hbm] * 6,
        out_specs=(anywhere, anywhere, anywhere),
        scratch_shapes=[
            V(blocks, bf16), V((rows, width), f32), V((rows, width), f32), V((rows, 2 * width), f32),
            V((rows, width), bf16), V(blocks, bf16), V(blocks, bf16), V((3, 32, 128), i32),
            V((8, 4, 128), i32), V((8, 4, 128), i32), V((32, 1, 128), i32), V((32, 1, 128), i32),
            V((256, 512), bf16),
            DMA, DMA, DMA, DMA((3,)), DMA, DMA, DMA, pltpu.SemaphoreType.REGULAR,
            DMA, DMA, DMA, DMA, DMA, DMA((8,)), DMA, DMA,
        ],
        compiler_params=pltpu.CompilerParams(
            collective_id=1, has_side_effects=True, vmem_limit_bytes=48 << 20
        ),
    )(
        deltas.reshape(blocks), row_ids.reshape(small), sample_counts.reshape(small),
        live.reshape(small), table, accum,
    )
    return new_table, new_accum, fresh.reshape(-1, width)


def solution(mesh):
    rows, slots = P(("aa", "ba"), None), P(("aa", "ba"))
    return jax.shard_map(
        on_device,
        mesh=mesh,
        in_specs=(rows, slots, slots, slots, rows, rows),
        out_specs=(rows, rows, rows),
        check_vma=False,
    )
```

time: 105 us -> 83.6 us (0.80)
  Pallas kernels: 96.2 us -> 74.5 us
    pallas_call x1, Pallas kernels: 96.2 us -> 74.5 us  [on_device(): pl.pallas_call(kernel, name='exchange', out_shape=(jax.ShapeDtypeStruct((...]
where the time goes in v2:
time: 83.6 us; the launch traced here: 83.2 us
  Pallas kernels  74.5 us (89%)
  local copies, waits for them, and re-layouts  8 us (10%)
    pallas_call x1, Pallas kernels, on_device(): pl.pallas_call(kernel, name='exchange', out_shape=(jax.ShapeDtypeStruct((...  74.5 us
    unnamed x13, local copies, waits for them, and re-layouts  8 us

profile of v2, /device:TPU:1, one launch (start us, length us, event | category | flops | bytes accessed | tf_op | source)
XLA Modules:
  0.0 83.2 jit_solution(16813480843740837389)
XLA Ops:
  0.6 0.0 copy-start
  0.6 1.2 %copy-done = bf16[4096,128]{1,0:T(8,128)(2,1)S(1)} copy-done((bf16[4096,128]{1,0:T(8,128)(2,1)S(1)}, bf16[4096,128]{1,0:T(8,128)(2,1)}, u32[]{:S(2)}) %copy-start) | copy-done | bytes 1048600
  1.9 0.0 copy-start.1
  1.9 0.7 copy-done.1
  2.6 0.0 copy-start.2
  2.6 0.7 copy-done.2
  3.3 0.0 copy-start.3
  3.3 0.7 copy-done.3
  4.0 74.5 %exchange.1 = (f32[4096,128]{1,0:T(8,128)S(1)}, f32[4096,128]{1,0:T(8,128)}, bf16[256,16,128]{2,1,0:T(8,128)(2,1)S(1)}) custom-call(bf16[256,16,128]{2,1,0:T(8,128)(2,1)S(1)} %bitcast.5, s32[32,128]{1,0:T(8,128)S(1)} %bitcast.7, s32[32,128]{1,0:T(8,128)S(1)} %bitcast.8, s32[32,128]{1,0:T(8,128)S(1)} %bitcast.9, f32[4096,128]{1,0:T(8,128)} %table.1, ...), custom_call_target="tpu_custom_call" | custom-call | tf_op jit(solution)/shard_map/exchange/pallas_call | solution.py:244
  78.5 0.0 copy-start.4
  78.5 1.3 %copy.12 = f32[4096,128]{1,0:T(8,128)} copy(f32[4096,128]{1,0:T(8,128)S(1)} %get-tuple-element.12) | data formatting | bytes 4194304
  79.9 1.0 %copy-done.4 = f32[4096,128]{1,0:T(8,128)S(1)} copy-done((f32[4096,128]{1,0:T(8,128)S(1)}, f32[4096,128]{1,0:T(8,128)}, u32[]{:S(2)}) %copy-start.4) | copy-done | bytes 2097176
  80.9 1.3 %copy.13 = f32[4096,128]{1,0:T(8,128)} copy(f32[4096,128]{1,0:T(8,128)S(1)} %copy-done.4) | data formatting | bytes 4194304
  82.2 1.0 %copy.14 = bf16[4096,128]{1,0:T(8,128)(2,1)} copy(bf16[4096,128]{1,0:T(8,128)(2,1)S(1)} %bitcast.6) | data formatting | bytes 2097152
Async XLA Ops:
  0.6 1.2 %copy-start = (bf16[4096,128]{1,0:T(8,128)(2,1)S(1)}, bf16[4096,128]{1,0:T(8,128)(2,1)}, u32[]{:S(2)}) copy-start(bf16[4096,128]{1,0:T(8,128)(2,1)} %param.6) | copy-start | bytes 3145732
  1.9 0.7 copy-start.1
  2.6 0.7 copy-start.2
  3.3 0.7 copy-start.3
  78.5 2.3 %copy-start.4 = (f32[4096,128]{1,0:T(8,128)S(1)}, f32[4096,128]{1,0:T(8,128)}, u32[]{:S(2)}) copy-start(f32[4096,128]{1,0:T(8,128)} %get-tuple-element.13) | copy-start | bytes 6291460

commit v3 on v2

--- a/solution.py
+++ b/solution.py
@@ -47,9 +47,9 @@
 
 def kernel(
     deltas, ids, counts, live, table, accum,
-    new_table, new_accum, fresh,
-    src, tab, acc, numer, upper, got, rep, ints, id_src, id_mid, id_row, id_got, lows,
-    in_sem, tab_sem, acc_sem, int_sem, tab_out, acc_out, own_sem, ready,
+    tab, acc, fresh,
+    src, numer, upper, got, rep, ints, id_src, id_mid, id_row, id_got, lows,
+    in_sem, tab_sem, acc_sem, int_sem, own_sem, ready,
     id_zsend, id_zrecv, id_bsend, id_brecv, dsend, drecv, rsend, rrecv,
 ):
     a, b = lax.axis_index("aa"), lax.axis_index("ba")
@@ -92,8 +92,9 @@
     id_mid[0] = id_src[a]
 
     def deltas_to(k, p):
+        group = k // 4 + k // 30
         pa, pb = (a + offset(p) + 8) % 8, partner(b, k)
-        send(src.at[32 * pa + pb], got.at[8 * k + p], dsend, drecv.at[k // 4], pa, pb)
+        send(src.at[32 * pa + pb], got.at[8 * k + p], dsend, drecv.at[group], pa, pb)
 
     def plane_near(p, _):
         deltas_to(0, p)
@@ -105,11 +106,11 @@
     pl.semaphore_wait(ready, 7)
 
     def plane(k, _):
-        for p in (1, 2, 3, 4, 5, 6, 7, 0):
+        for p in (7, 5, 6, 3, 4, 1, 2, 0):
             deltas_to(k, p)
         return 0
 
-    lax.fori_loop(1, 4, plane, 0)
+    lax.fori_loop(1, 10, plane, 0)
     landed(id_mid.at[pl.ds(1, 7)], id_zrecv)
     for r in range(4):
         id_row[8 * r : 8 * r + 8, 0, :] = swap_blocks(id_mid[:, r, :])
@@ -121,52 +122,56 @@
 
     lax.fori_loop(1, 32, ids_across, 0)
     id_got[0] = id_row[b]
-    lax.fori_loop(4, 32, plane, 0)
+    lax.fori_loop(10, 32, plane, 0)
     numer[...] = jnp.zeros_like(numer)
     landed(id_got.at[pl.ds(0, 31)], id_brecv)
 
-    def scatter(g, count):
-        landed(got.at[pl.ds(0, count)], drecv.at[g])
-        lanes = [id_got[4 * g + i] for i in range(4)]
-        both = jnp.concatenate(lanes, axis=1)
+    def arrived(k, n, count, group):
+        landed(got.at[pl.ds(0, count)], drecv.at[group])
+        width = 128 * n
+        both = jnp.concatenate([id_got[k + i] for i in range(n)], axis=1)
         row = both % 65536
-        high = row // 256
         weight = (both // 65536).astype(jnp.float32)
-        low = lax.broadcasted_iota(jnp.int32, (256, 512), 0) == row % 256
-        lows[...] = jnp.where(low, 1.0, 0.0).astype(jnp.bfloat16)
-        values = got[pl.ds(32 * g, 32)].reshape(512, 128)
-        values = jnp.concatenate([values, jnp.ones_like(values)], axis=1)
+        low = lax.broadcasted_iota(jnp.int32, (256, width), 0) == row % 256
+        lows[:, 0:width] = jnp.where(low, 1.0, 0.0).astype(jnp.bfloat16)
+        values = got[pl.ds(8 * k, 8 * n)].reshape(width, 128)
+        return row // 256, weight, jnp.concatenate([values, jnp.ones_like(values)], axis=1)
+
+    def partial(high, weight, values, i):
+        width = values.shape[0]
+        picks = []
+        for j in range(STEP // 256):
+            w = jnp.where(high == i * (STEP // 256) + j, weight, 0.0)
+            w = jnp.broadcast_to(w, (16, width)).astype(jnp.bfloat16)
+            picks.append(lows[:, 0:width] * jnp.concatenate([w] * 16, axis=0))
+        return jnp.dot(jnp.concatenate(picks, axis=0), values, preferred_element_type=jnp.float32)
+
+    def scatter(k, n, count, group):
+        slots = arrived(k, n, count, group)
 
         def block(i, _):
-            base = pl.multiple_of(i * STEP, STEP)
-            picks = []
-            for j in range(STEP // 256):
-                w = jnp.where(high == i * (STEP // 256) + j, weight, 0.0)
-                w = jnp.broadcast_to(w, (16, 512)).astype(jnp.bfloat16)
-                w = jnp.concatenate([w] * 16, axis=0)
-                picks.append(lows[...] * w)
-            numer[pl.ds(base, STEP), :] += jnp.dot(
-                jnp.concatenate(picks, axis=0), values, preferred_element_type=jnp.float32
-            )
+            numer[pl.ds(pl.multiple_of(i * STEP, STEP), STEP), :] += partial(*slots, i)
             return 0
 
         lax.fori_loop(0, rows // STEP, block, 0)
 
     own.wait()
-    scatter(0, 31)
+    scatter(0, 4, 31, 0)
 
     def incoming(g, _):
-        scatter(g, 32)
-        return 0
-
-    lax.fori_loop(1, 8, incoming, 0)
-
+        scatter(4 * g, 4, 32, g)
+        return 0
+
+    lax.fori_loop(1, 7, incoming, 0)
+    scatter(28, 2, 16, 7)
     load_tab.wait()
     load_acc.wait()
+    last = arrived(30, 2, 16, 8)
 
     def update(i, _):
-        at = pl.ds(pl.multiple_of(i * 256, 256), 256)
-        grad = numer[at, 0:128] / jnp.maximum(numer[at, 128:256], 1.0)
+        at = pl.ds(pl.multiple_of(i * STEP, STEP), STEP)
+        sums = numer[at, :] + partial(*last, i)
+        grad = sums[:, 0:128] / jnp.maximum(sums[:, 128:256], 1.0)
         accum_next = acc[at, :] + grad * grad
         table_next = tab[at, :] - learn_rate * grad / (jnp.sqrt(accum_next) + epsilon)
         acc[at, :] = accum_next
@@ -174,15 +179,13 @@
         upper[at, :] = table_next.astype(jnp.bfloat16)
         return 0
 
-    lax.fori_loop(0, rows // 256, update, 0)
-    store_tab = pltpu.make_async_copy(tab, new_table, tab_out)
-    store_acc = pltpu.make_async_copy(acc, new_accum, acc_out)
-
-    def gather(g):
-        columns = [jnp.broadcast_to(id_got[4 * g + i] % 65536, (128, 128)).T for i in range(4)]
+    lax.fori_loop(0, rows // STEP, update, 0)
+
+    def gather(k, n):
+        columns = [jnp.broadcast_to(id_got[k + i] % 65536, (128, 128)).T for i in range(n)]
         row = jnp.concatenate(columns, axis=0)
         high = (row // 256).astype(jnp.float32).astype(jnp.bfloat16)
-        lane = lax.broadcasted_iota(jnp.int32, (512, 128), 1)
+        lane = lax.broadcasted_iota(jnp.int32, row.shape, 1)
         row = row % 256
         near = jnp.where(row == lane, 1.0, 0.0).astype(jnp.bfloat16)
         far = jnp.where(row == lane + 128, 1.0, 0.0).astype(jnp.bfloat16)
@@ -193,28 +196,27 @@
             [jnp.where(high == float(k), low, zero) for k in range(rows // 256)], axis=1
         )
         total = jnp.dot(picks, upper[...], preferred_element_type=jnp.float32)
-        rep[pl.ds(32 * g, 32)] = total.astype(jnp.bfloat16).reshape(32, 16, 128)
+        rep[pl.ds(8 * k, 8 * n)] = total.astype(jnp.bfloat16).reshape(8 * n, 16, 128)
 
     def reply(k, p):
         pa, pb = (a - offset(p) + 8) % 8, partner_back(b, k)
         send(rep.at[8 * k + p], fresh.at[me], rsend, rrecv, pa, pb)
 
     def replies(k, _):
-        for p in (1, 2, 3, 4, 5, 6, 7, 0):
+        for p in (7, 5, 6, 3, 4, 1, 2, 0):
             reply(k, p)
         return 0
 
-    gather(0)
+    gather(0, 1)
+    for p in range(7, 0, -1):
+        reply(0, p)
     back = pltpu.make_async_copy(rep.at[0], fresh.at[me], own_sem)
     back.start()
-    for p in range(1, 8):
-        reply(0, p)
+    gather(1, 3)
     lax.fori_loop(1, 4, replies, 0)
-    store_tab.start()
-    store_acc.start()
 
     def outgoing(g, _):
-        gather(g)
+        gather(4 * g, 4)
         lax.fori_loop(4 * g, 4 * g + 4, replies, 0)
         return 0
 
@@ -226,18 +228,27 @@
     landed(got.at[pl.ds(0, 255)], dsend)
     landed(rep.at[pl.ds(0, 255)], rsend)
     landed(fresh.at[pl.ds(0, 255)], rrecv)
-    store_tab.wait()
-    store_acc.wait()
 
 
 STEP = 1024
+LIMIT = 46
+
+
+def write_out(a, b, c, a_out, b_out, c_out, *sems):
+    copies = [
+        pltpu.make_async_copy(x, y, sem) for x, y, sem in zip((a, b, c), (a_out, b_out, c_out), sems)
+    ]
+    for copy in copies:
+        copy.start()
+    for copy in copies:
+        copy.wait()
 
 
 def on_device(deltas, row_ids, sample_counts, live, table, accum):
     rows, width = table.shape
     blocks = (256, 16, width)
     small = (32, 128)
-    anywhere = pl.BlockSpec(memory_space=pl.ANY)
+    vmem = pl.BlockSpec(memory_space=pltpu.VMEM)
     hbm = pl.BlockSpec(memory_space=pltpu.HBM)
     bf16, f32, i32 = jnp.bfloat16, jnp.float32, jnp.int32
     V = pltpu.VMEM
@@ -250,22 +261,36 @@
             jax.ShapeDtypeStruct(blocks, bf16),
         ),
         in_specs=[hbm] * 6,
-        out_specs=(anywhere, anywhere, anywhere),
+        out_specs=(vmem, vmem, vmem),
         scratch_shapes=[
-            V(blocks, bf16), V((rows, width), f32), V((rows, width), f32), V((rows, 2 * width), f32),
+            V(blocks, bf16), V((rows, 2 * width), f32),
             V((rows, width), bf16), V(blocks, bf16), V(blocks, bf16), V((3, 32, 128), i32),
             V((8, 4, 128), i32), V((8, 4, 128), i32), V((32, 1, 128), i32), V((32, 1, 128), i32),
             V((256, 512), bf16),
-            DMA, DMA, DMA, DMA((3,)), DMA, DMA, DMA, pltpu.SemaphoreType.REGULAR,
-            DMA, DMA, DMA, DMA, DMA, DMA((8,)), DMA, DMA,
+            DMA, DMA, DMA, DMA((3,)), DMA, pltpu.SemaphoreType.REGULAR,
+            DMA, DMA, DMA, DMA, DMA, DMA((9,)), DMA, DMA,
         ],
         compiler_params=pltpu.CompilerParams(
-            collective_id=1, has_side_effects=True, vmem_limit_bytes=48 << 20
+            collective_id=1, has_side_effects=True, vmem_limit_bytes=LIMIT << 20
         ),
     )(
+        *(pltpu.with_memory_space_constraint(x, pltpu.HBM) for x in (
         deltas.reshape(blocks), row_ids.reshape(small), sample_counts.reshape(small),
-        live.reshape(small), table, accum,
+        live.reshape(small), table, accum)),
     )
+    new_table, new_accum, fresh = pl.pallas_call(
+        write_out,
+        name="write_out",
+        out_shape=(
+            jax.ShapeDtypeStruct((rows, width), f32),
+            jax.ShapeDtypeStruct((rows, width), f32),
+            jax.ShapeDtypeStruct(blocks, bf16),
+        ),
+        in_specs=[vmem] * 3,
+        out_specs=(hbm, hbm, hbm),
+        scratch_shapes=[DMA, DMA, DMA],
+        compiler_params=pltpu.CompilerParams(vmem_limit_bytes=2 << 20),
+    )(*(pltpu.with_memory_space_constraint(x, pltpu.VMEM) for x in (new_table, new_accum, fresh)))
     return new_table, new_accum, fresh.reshape(-1, width)
 
 

time: 83.6 us -> 76.6 us (0.916)
  local copies, waits for them, and re-layouts: 8 us -> 0 us
  Pallas kernels: 74.5 us -> 75.9 us
    unnamed x13 -> x0, local copies, waits for them, and re-layouts: 8 us -> none
    pallas_call x0 -> x1, Pallas kernels: none -> 2.38 us  [on_device(): pl.pallas_call(write_out, name='write_out', out_shape=(jax.ShapeDtypeStru...]
    pallas_call x1, Pallas kernels: 74.5 us -> 73.5 us  [on_device(): pl.pallas_call(kernel, name='exchange', out_shape=(jax.ShapeDtypeStruct((...]
where the time goes in v3:
time: 76.6 us
  Pallas kernels  75.9 us (99%)
    pallas_call x1, Pallas kernels, on_device(): pl.pallas_call(kernel, name='exchange', out_shape=(jax.ShapeDtypeStruct((...  73.5 us
    pallas_call x1, Pallas kernels, on_device(): pl.pallas_call(write_out, name='write_out', out_shape=(jax.ShapeDtypeStru...  2.38 us

profile of v3, /device:TPU:1, one launch (start us, length us, event | category | flops | bytes accessed | tf_op | source)
XLA Modules:
  0.0 76.6 jit_solution(6636205071659711909)
XLA Ops:
  0.6 73.5 %exchange.1 = (f32[4096,128]{1,0:T(8,128)S(1)}, f32[4096,128]{1,0:T(8,128)S(1)}, bf16[256,16,128]{2,1,0:T(8,128)(2,1)S(1)}) custom-call(bf16[256,16,128]{2,1,0:T(8,128)(2,1)} %bitcast.5, s32[32,128]{1,0:T(8,128)} %bitcast.6, s32[32,128]{1,0:T(8,128)} %bitcast.7, s32[32,128]{1,0:T(8,128)} %bitcast.8, f32[4096,128]{1,0:T(8,128)} %table.1, f32[4096,128]{1,0:T(8,128)} %accum.1), custom_call_target="tpu_custom_call" | custom-call | tf_op jit(solution)/shard_map/exchange/pallas_call | solution.py:255
  74.2 2.4 %write_out.1 = (f32[4096,128]{1,0:T(8,128)}, f32[4096,128]{1,0:T(8,128)}, bf16[256,16,128]{2,1,0:T(8,128)(2,1)}) custom-call(f32[4096,128]{1,0:T(8,128)S(1)} %get-tuple-element.9.a, f32[4096,128]{1,0:T(8,128)S(1)} %get-tuple-element.10.b, bf16[256,16,128]{2,1,0:T(8,128)(2,1)S(1)} %get-tuple-element.11.c), custom_call_target="tpu_custom_call" | custom-call | tf_op jit(solution)/shard_map/write_out/pallas_call | solution.py:281

commit v4 on v3

--- a/solution.py
+++ b/solution.py
@@ -48,7 +48,7 @@
 def kernel(
     deltas, ids, counts, live, table, accum,
     tab, acc, fresh,
-    src, numer, upper, got, rep, ints, id_src, id_mid, id_row, id_got, lows,
+    src, numer, inverse, totals, first, upper, got, rep, ints, id_src, id_mid, id_row, id_got, lows,
     in_sem, tab_sem, acc_sem, int_sem, own_sem, ready,
     id_zsend, id_zrecv, id_bsend, id_brecv, dsend, drecv, rsend, rrecv,
 ):
@@ -68,11 +68,8 @@
     for d in range(1, 8):
         pl.semaphore_signal(barrier, inc=1, device_id=((a + d) % 8, b), device_id_type=MESH)
 
-    def greet(k, _):
+    for k in range(1, 32):
         pl.semaphore_signal(barrier, inc=1, device_id=(a, partner(b, k)), device_id_type=MESH)
-        return 0
-
-    lax.fori_loop(1, 32, greet, 0)
     for copy in load_ints:
         copy.wait()
     packed = ints[0] + ints[1] * ints[2] * 65536
@@ -124,64 +121,54 @@
     id_got[0] = id_row[b]
     lax.fori_loop(10, 32, plane, 0)
     numer[...] = jnp.zeros_like(numer)
+    totals[...] = jnp.zeros_like(totals)
     landed(id_got.at[pl.ds(0, 31)], id_brecv)
 
-    def arrived(k, n, count, group):
-        landed(got.at[pl.ds(0, count)], drecv.at[group])
+    def weights(k, n):
         width = 128 * n
         both = jnp.concatenate([id_got[k + i] for i in range(n)], axis=1)
         row = both % 65536
         weight = (both // 65536).astype(jnp.float32)
         low = lax.broadcasted_iota(jnp.int32, (256, width), 0) == row % 256
         lows[:, 0:width] = jnp.where(low, 1.0, 0.0).astype(jnp.bfloat16)
-        values = got[pl.ds(8 * k, 8 * n)].reshape(width, 128)
-        return row // 256, weight, jnp.concatenate([values, jnp.ones_like(values)], axis=1)
-
-    def partial(high, weight, values, i):
+        return row // 256, weight
+
+    def add_totals(g, _):
+        high, weight = weights(4 * g, 4)
+        here = lax.broadcasted_iota(jnp.int32, (rows // 256, 512), 0) == high
+        totals[...] += lax.dot_general(
+            jnp.where(here, weight, 0.0).astype(jnp.bfloat16),
+            lows[...],
+            (((1,), (1,)), ((), ())),
+            preferred_element_type=jnp.float32,
+        )
+        return 0
+
+    def partial(high, weight, values, i, step):
         width = values.shape[0]
         picks = []
-        for j in range(STEP // 256):
-            w = jnp.where(high == i * (STEP // 256) + j, weight, 0.0)
+        for j in range(step // 256):
+            w = jnp.where(high == i * (step // 256) + j, weight, 0.0)
             w = jnp.broadcast_to(w, (16, width)).astype(jnp.bfloat16)
             picks.append(lows[:, 0:width] * jnp.concatenate([w] * 16, axis=0))
         return jnp.dot(jnp.concatenate(picks, axis=0), values, preferred_element_type=jnp.float32)
 
+    def arrived(k, n, count, group):
+        landed(got.at[pl.ds(0, count)], drecv.at[group])
+        return got[pl.ds(8 * k, 8 * n)].reshape(128 * n, 128)
+
     def scatter(k, n, count, group):
-        slots = arrived(k, n, count, group)
+        high, weight = weights(k, n)
+        values = arrived(k, n, count, group)
 
         def block(i, _):
-            numer[pl.ds(pl.multiple_of(i * STEP, STEP), STEP), :] += partial(*slots, i)
+            at = pl.ds(pl.multiple_of(i * STEP, STEP), STEP)
+            numer[at, :] += partial(high, weight, values, i, STEP)
             return 0
 
         lax.fori_loop(0, rows // STEP, block, 0)
 
-    own.wait()
-    scatter(0, 4, 31, 0)
-
-    def incoming(g, _):
-        scatter(4 * g, 4, 32, g)
-        return 0
-
-    lax.fori_loop(1, 7, incoming, 0)
-    scatter(28, 2, 16, 7)
-    load_tab.wait()
-    load_acc.wait()
-    last = arrived(30, 2, 16, 8)
-
-    def update(i, _):
-        at = pl.ds(pl.multiple_of(i * STEP, STEP), STEP)
-        sums = numer[at, :] + partial(*last, i)
-        grad = sums[:, 0:128] / jnp.maximum(sums[:, 128:256], 1.0)
-        accum_next = acc[at, :] + grad * grad
-        table_next = tab[at, :] - learn_rate * grad / (jnp.sqrt(accum_next) + epsilon)
-        acc[at, :] = accum_next
-        tab[at, :] = table_next
-        upper[at, :] = table_next.astype(jnp.bfloat16)
-        return 0
-
-    lax.fori_loop(0, rows // STEP, update, 0)
-
-    def gather(k, n):
+    def one_hot(k, n):
         columns = [jnp.broadcast_to(id_got[k + i] % 65536, (128, 128)).T for i in range(n)]
         row = jnp.concatenate(columns, axis=0)
         high = (row // 256).astype(jnp.float32).astype(jnp.bfloat16)
@@ -192,9 +179,44 @@
         low = jnp.concatenate([near, far], axis=1)
         high = jnp.concatenate([high, high], axis=1)
         zero = jnp.zeros_like(low)
-        picks = jnp.concatenate(
+        return jnp.concatenate(
             [jnp.where(high == float(k), low, zero) for k in range(rows // 256)], axis=1
         )
+
+    lax.fori_loop(0, 8, add_totals, 0)
+    inv = 1.0 / jnp.maximum(totals[...], 1.0)
+    for h in range(rows // 256):
+        inverse[256 * h : 256 * h + 256, :] = jnp.broadcast_to(inv[h : h + 1, :], (128, 256)).T
+    first[...] = one_hot(0, 1)
+
+    own.wait()
+    scatter(0, 4, 31, 0)
+
+    def incoming(g, _):
+        scatter(4 * g, 4, 32, g)
+        return 0
+
+    lax.fori_loop(1, 7, incoming, 0)
+    scatter(28, 2, 16, 7)
+
+    high, weight = weights(30, 2)
+    load_tab.wait()
+    load_acc.wait()
+    values = arrived(30, 2, 16, 8)
+
+    def update(i, _):
+        at = pl.ds(pl.multiple_of(i * USTEP, USTEP), USTEP)
+        grad = (numer[at, :] + partial(high, weight, values, i, USTEP)) * inverse[at, :]
+        accum_next = acc[at, :] + grad * grad
+        table_next = tab[at, :] - learn_rate * grad / (jnp.sqrt(accum_next) + epsilon)
+        acc[at, :] = accum_next
+        tab[at, :] = table_next
+        upper[at, :] = table_next.astype(jnp.bfloat16)
+        return 0
+
+    lax.fori_loop(0, rows // USTEP, update, 0)
+
+    def gather(k, n, picks):
         total = jnp.dot(picks, upper[...], preferred_element_type=jnp.float32)
         rep[pl.ds(8 * k, 8 * n)] = total.astype(jnp.bfloat16).reshape(8 * n, 16, 128)
 
@@ -207,16 +229,16 @@
             reply(k, p)
         return 0
 
-    gather(0, 1)
+    gather(0, 1, first[...])
     for p in range(7, 0, -1):
         reply(0, p)
     back = pltpu.make_async_copy(rep.at[0], fresh.at[me], own_sem)
     back.start()
-    gather(1, 3)
+    gather(1, 3, one_hot(1, 3))
     lax.fori_loop(1, 4, replies, 0)
 
     def outgoing(g, _):
-        gather(4 * g, 4)
+        gather(4 * g, 4, one_hot(4 * g, 4))
         lax.fori_loop(4 * g, 4 * g + 4, replies, 0)
         return 0
 
@@ -230,7 +252,8 @@
     landed(fresh.at[pl.ds(0, 255)], rrecv)
 
 
-STEP = 1024
+STEP = 2048
+USTEP = 2048
 LIMIT = 46
 
 
@@ -263,7 +286,8 @@
         in_specs=[hbm] * 6,
         out_specs=(vmem, vmem, vmem),
         scratch_shapes=[
-            V(blocks, bf16), V((rows, 2 * width), f32),
+            V(blocks, bf16), V((rows, width), f32), V((rows, width), f32),
+            V((rows // 256, 256), f32), V((width, rows), bf16),
             V((rows, width), bf16), V(blocks, bf16), V(blocks, bf16), V((3, 32, 128), i32),
             V((8, 4, 128), i32), V((8, 4, 128), i32), V((32, 1, 128), i32), V((32, 1, 128), i32),
             V((256, 512), bf16),

time: 76.6 us -> 75 us (0.979)
  Pallas kernels: 75.9 us -> 74.2 us
    pallas_call x1, Pallas kernels: 73.5 us -> 71.8 us  [on_device(): pl.pallas_call(kernel, name='exchange', out_shape=(jax.ShapeDtypeStruct((...]
where the time goes in v4:
time: 75 us; the launch traced here: 74.9 us
  Pallas kernels  74.2 us (99%)
    pallas_call x1, Pallas kernels, on_device(): pl.pallas_call(kernel, name='exchange', out_shape=(jax.ShapeDtypeStruct((...  71.8 us
    pallas_call x1, Pallas kernels, on_device(): pl.pallas_call(write_out, name='write_out', out_shape=(jax.ShapeDtypeStru...  2.38 us

profile of v4, /device:TPU:1, one launch (start us, length us, event | category | flops | bytes accessed | tf_op | source)
XLA Modules:
  0.0 74.9 jit_solution(8215330563048207770)
XLA Ops:
  0.6 71.8 %exchange.1 = (f32[4096,128]{1,0:T(8,128)S(1)}, f32[4096,128]{1,0:T(8,128)S(1)}, bf16[256,16,128]{2,1,0:T(8,128)(2,1)S(1)}) custom-call(bf16[256,16,128]{2,1,0:T(8,128)(2,1)} %bitcast.5, s32[32,128]{1,0:T(8,128)} %bitcast.6, s32[32,128]{1,0:T(8,128)} %bitcast.7, s32[32,128]{1,0:T(8,128)} %bitcast.8, f32[4096,128]{1,0:T(8,128)} %table.1, f32[4096,128]{1,0:T(8,128)} %accum.1), custom_call_target="tpu_custom_call" | custom-call | tf_op jit(solution)/shard_map/exchange/pallas_call | solution.py:278
  72.5 2.4 %write_out.1 = (f32[4096,128]{1,0:T(8,128)}, f32[4096,128]{1,0:T(8,128)}, bf16[256,16,128]{2,1,0:T(8,128)(2,1)}) custom-call(f32[4096,128]{1,0:T(8,128)S(1)} %get-tuple-element.9.a, f32[4096,128]{1,0:T(8,128)S(1)} %get-tuple-element.10.b, bf16[256,16,128]{2,1,0:T(8,128)(2,1)S(1)} %get-tuple-element.11.c), custom_call_target="tpu_custom_call" | custom-call | tf_op jit(solution)/shard_map/write_out/pallas_call | solution.py:305

commit v5 on v4

--- a/solution.py
+++ b/solution.py
@@ -100,10 +100,16 @@
     own = pltpu.make_async_copy(src.at[me], got.at[0], own_sem)
     own.start()
     lax.fori_loop(1, 8, plane_near, 0)
+
+    def plane_far(k, _):
+        deltas_to(k, 0)
+        return 0
+
+    lax.fori_loop(1, 32, plane_far, 0)
     pl.semaphore_wait(ready, 7)
 
     def plane(k, _):
-        for p in (7, 5, 6, 3, 4, 1, 2, 0):
+        for p in (7, 5, 6, 3, 4, 1, 2):
             deltas_to(k, p)
         return 0
 

time: 75 us -> 75 us (level)
  no operation moved by 1% of the time
where the time goes in v5:
time: 75 us; the launch traced here: 74.9 us
  Pallas kernels  74.2 us (99%)
    pallas_call x1, Pallas kernels, on_device(): pl.pallas_call(kernel, name='exchange', out_shape=(jax.ShapeDtypeStruct((...  71.9 us
    pallas_call x1, Pallas kernels, on_device(): pl.pallas_call(write_out, name='write_out', out_shape=(jax.ShapeDtypeStru...  2.38 us

profile of v5, /device:TPU:1, one launch (start us, length us, event | category | flops | bytes accessed | tf_op | source)
XLA Modules:
  0.0 74.9 jit_solution(11437420575898168915)
XLA Ops:
  0.6 71.9 %exchange.1 = (f32[4096,128]{1,0:T(8,128)S(1)}, f32[4096,128]{1,0:T(8,128)S(1)}, bf16[256,16,128]{2,1,0:T(8,128)(2,1)S(1)}) custom-call(bf16[256,16,128]{2,1,0:T(8,128)(2,1)} %bitcast.5, s32[32,128]{1,0:T(8,128)} %bitcast.6, s32[32,128]{1,0:T(8,128)} %bitcast.7, s32[32,128]{1,0:T(8,128)} %bitcast.8, f32[4096,128]{1,0:T(8,128)} %table.1, f32[4096,128]{1,0:T(8,128)} %accum.1), custom_call_target="tpu_custom_call" | custom-call | tf_op jit(solution)/shard_map/exchange/pallas_call | solution.py:284
  72.5 2.4 %write_out.1 = (f32[4096,128]{1,0:T(8,128)}, f32[4096,128]{1,0:T(8,128)}, bf16[256,16,128]{2,1,0:T(8,128)(2,1)}) custom-call(f32[4096,128]{1,0:T(8,128)S(1)} %get-tuple-element.9.a, f32[4096,128]{1,0:T(8,128)S(1)} %get-tuple-element.10.b, bf16[256,16,128]{2,1,0:T(8,128)(2,1)S(1)} %get-tuple-element.11.c), custom_call_target="tpu_custom_call" | custom-call | tf_op jit(solution)/shard_map/write_out/pallas_call | solution.py:311

commit v6 on v5

--- a/solution.py
+++ b/solution.py
@@ -48,7 +48,7 @@
 def kernel(
     deltas, ids, counts, live, table, accum,
     tab, acc, fresh,
-    src, numer, inverse, totals, first, upper, got, rep, ints, id_src, id_mid, id_row, id_got, lows,
+    src, numer, inverse, totals, first, second, upper, got, rep, ints, id_src, id_mid, id_row, id_got, lows,
     in_sem, tab_sem, acc_sem, int_sem, own_sem, ready,
     id_zsend, id_zrecv, id_bsend, id_brecv, dsend, drecv, rsend, rrecv,
 ):
@@ -194,6 +194,7 @@
     for h in range(rows // 256):
         inverse[256 * h : 256 * h + 256, :] = jnp.broadcast_to(inv[h : h + 1, :], (128, 256)).T
     first[...] = one_hot(0, 1)
+    second[...] = one_hot(1, 3)
 
     own.wait()
     scatter(0, 4, 31, 0)
@@ -240,7 +241,7 @@
         reply(0, p)
     back = pltpu.make_async_copy(rep.at[0], fresh.at[me], own_sem)
     back.start()
-    gather(1, 3, one_hot(1, 3))
+    gather(1, 3, second[...])
     lax.fori_loop(1, 4, replies, 0)
 
     def outgoing(g, _):
@@ -293,7 +294,7 @@
         out_specs=(vmem, vmem, vmem),
         scratch_shapes=[
             V(blocks, bf16), V((rows, width), f32), V((rows, width), f32),
-            V((rows // 256, 256), f32), V((width, rows), bf16),
+            V((rows // 256, 256), f32), V((width, rows), bf16), V((3 * width, rows), bf16),
             V((rows, width), bf16), V(blocks, bf16), V(blocks, bf16), V((3, 32, 128), i32),
             V((8, 4, 128), i32), V((8, 4, 128), i32), V((32, 1, 128), i32), V((32, 1, 128), i32),
             V((256, 512), bf16),

time: 75 us -> 75 us (level)
  no operation moved by 1% of the time
where the time goes in v6:
time: 75 us; the launch traced here: 74.8 us
  Pallas kernels  74.1 us (99%)
    pallas_call x1, Pallas kernels, on_device(): pl.pallas_call(kernel, name='exchange', out_shape=(jax.ShapeDtypeStruct((...  71.8 us
    pallas_call x1, Pallas kernels, on_device(): pl.pallas_call(write_out, name='write_out', out_shape=(jax.ShapeDtypeStru...  2.38 us

profile of v6, /device:TPU:1, one launch (start us, length us, event | category | flops | bytes accessed | tf_op | source)
XLA Modules:
  0.0 74.8 jit_solution(907239141292504302)
XLA Ops:
  0.6 71.8 %exchange.1 = (f32[4096,128]{1,0:T(8,128)S(1)}, f32[4096,128]{1,0:T(8,128)S(1)}, bf16[256,16,128]{2,1,0:T(8,128)(2,1)S(1)}) custom-call(bf16[256,16,128]{2,1,0:T(8,128)(2,1)} %bitcast.5, s32[32,128]{1,0:T(8,128)} %bitcast.6, s32[32,128]{1,0:T(8,128)} %bitcast.7, s32[32,128]{1,0:T(8,128)} %bitcast.8, f32[4096,128]{1,0:T(8,128)} %table.1, f32[4096,128]{1,0:T(8,128)} %accum.1), custom_call_target="tpu_custom_call" | custom-call | tf_op jit(solution)/shard_map/exchange/pallas_call | solution.py:285
  72.4 2.4 %write_out.1 = (f32[4096,128]{1,0:T(8,128)}, f32[4096,128]{1,0:T(8,128)}, bf16[256,16,128]{2,1,0:T(8,128)(2,1)}) custom-call(f32[4096,128]{1,0:T(8,128)S(1)} %get-tuple-element.9.a, f32[4096,128]{1,0:T(8,128)S(1)} %get-tuple-element.10.b, bf16[256,16,128]{2,1,0:T(8,128)(2,1)S(1)} %get-tuple-element.11.c), custom_call_target="tpu_custom_call" | custom-call | tf_op jit(solution)/shard_map/write_out/pallas_call | solution.py:312
